TPU v7x, 32 devices: a whole 2x2x4 slice. The times are simulated.
32 devices in a mesh: term: 8 (over z, core), doc: 4 (over y, x).
Axes of the slice: x: 2, y: 2, z: 4, core: 2. Of those that a mesh axis runs over, the one named last changes fastest.
Arguments:
- tile_values: bfloat16 [384, 512, 128], P('term', 'doc'), may hold values from 0.001 to 1, as said below
- tile_rows: int32 [8, 192], P('term', 'doc'), may hold values from 0 to 15, as said below
- tile_cols: int32 [8, 192], P('term', 'doc'), may hold values from 0 to 15, as said below
- tile_count: int32 [8, 4], P('term', 'doc'), may hold values from 16 to 48, as said below
- start_block: bfloat16 [8192, 256], P('doc'), may hold values from -6 to 6
Outputs:
- row_scale: float32 [16384], P('term')
- col_scale: float32 [8192], P('doc')
- left_basis: bfloat16 [16384, 256], P('term')
- right_basis: bfloat16 [8192, 256], P('doc')
Inputs may be any that keep to these rules, and one draw needn't show every extreme that they name: `tile_values`: entries are positive. `tile_rows`: within one block pair the occupied (row, column) pairs are distinct, and every tile row and tile column of every block pair holds an occupied tile. `tile_cols`: paired with tile_rows slot by slot. `tile_count`: some block pair has all 48 slots occupied.
All inputs are finite; a program needn't handle non-finite values.
Results may differ from a plain program's by a relative error of at most 0.006.
The roundings to bfloat16 on the way count: a program that leaves them out, or rounds other values in their place, can miss the bound.
Values may be sent and summed in bfloat16 or wider, within the bound.
A program may use at most 64 MiB of HBM per device.

v0:
```python
import math
import jax
import jax.numpy as jnp
from jax import lax
from jax.sharding import PartitionSpec as P

TILE = 128
K = 256
PASSES = 2
RB = 16
CB = 16
PRECISE = lax.Precision.HIGHEST


def factor_inverse(gram):
    lower = jnp.linalg.cholesky(gram)
    identity = jnp.eye(gram.shape[0], dtype=gram.dtype)
    return jax.scipy.linalg.solve_triangular(lower, identity, lower=True).T


def over_tiles(tile_values, row_ids, col_ids, occupied, advance, initial):
    slot_total = tile_values.shape[0]
    group_size = math.gcd(slot_total, 32)

    def visit(turn_index, running):
        offset = turn_index * group_size
        tile_block = lax.dynamic_slice_in_dim(tile_values, offset, group_size, 0)
        row_block = lax.dynamic_slice_in_dim(row_ids, offset, group_size, 0)
        col_block = lax.dynamic_slice_in_dim(col_ids, offset, group_size, 0)
        live_mask = (offset + jnp.arange(group_size, dtype=jnp.int32) < occupied).astype(
            jnp.float32
        )
        return advance(running, tile_block, row_block, col_block, live_mask)

    turn_total = slot_total // group_size
    return lax.fori_loop(0, turn_total, visit, initial)


def row_vector(source):

    def advance(running, tile_block, row_block, col_block, live_mask):
        picked = jnp.take(source, col_block, axis=0)
        product = jnp.einsum(
            "gab,gb->ga", tile_block.astype(jnp.float32), picked, precision=PRECISE
        )
        return running.at[row_block].add(product * live_mask[:, None])

    return advance


def col_vector(source):

    def advance(running, tile_block, row_block, col_block, live_mask):
        picked = jnp.take(source, row_block, axis=0)
        product = jnp.einsum(
            "gab,ga->gb", tile_block.astype(jnp.float32), picked, precision=PRECISE
        )
        return running.at[col_block].add(product * live_mask[:, None])

    return advance


def row_matrix(source):

    def advance(running, tile_block, row_block, col_block, live_mask):
        picked = jnp.take(source, col_block, axis=0)
        product = jnp.einsum("gab,gbk->gak", tile_block, picked, preferred_element_type=jnp.float32)
        return running.at[row_block].add(product * live_mask[:, None, None])

    return advance


def col_matrix(source):

    def advance(running, tile_block, row_block, col_block, live_mask):
        picked = jnp.take(source, row_block, axis=0)
        product = jnp.einsum("gab,gak->gbk", tile_block, picked, preferred_element_type=jnp.float32)
        return running.at[col_block].add(product * live_mask[:, None, None])

    return advance


def per_device(tile_values, tile_rows, tile_cols, tile_count, start_block):
    row_list = tile_rows[0]
    col_list = tile_cols[0]
    occupied = tile_count[0, 0]
    terms_total = RB * TILE * lax.axis_size("term")
    docs_total = CB * TILE * lax.axis_size("doc")

    def tile_pass(advance, initial):
        return over_tiles(tile_values, row_list, col_list, occupied, advance, initial)

    col_scale = jnp.ones((CB, TILE), jnp.float32)
    row_scale = jnp.ones((RB, TILE), jnp.float32)
    mean_part = jnp.sum(start_block.astype(jnp.float32), axis=0)
    start_mean = mean_part
    for sweep_index in range(PASSES):
        row_part = tile_pass(row_vector(col_scale), jnp.zeros((RB, TILE), jnp.float32))
        if sweep_index == 0:
            row_total, start_mean = lax.psum((row_part, mean_part), "doc")
        else:
            row_total = lax.psum(row_part, "doc")
        row_scale = 1.0 / row_total
        col_part = tile_pass(col_vector(row_scale), jnp.zeros((CB, TILE), jnp.float32))
        col_scale = 1.0 / lax.psum(col_part, "term")
    weight_part = tile_pass(row_vector(col_scale), jnp.zeros((RB, TILE), jnp.float32)).reshape(-1)
    row_flat = row_scale.reshape(-1)
    col_flat = col_scale.reshape(-1)
    scaled_start = (col_flat[:, None] * start_block.astype(jnp.float32)).astype(jnp.bfloat16)
    left_part = tile_pass(
        row_matrix(scaled_start.reshape(CB, TILE, K)), jnp.zeros((RB, TILE, K), jnp.float32)
    )
    left_part = left_part.reshape(RB * TILE, K)
    left_share = RB * TILE // lax.axis_size("doc")
    left_offset = lax.axis_index("doc") * left_share
    left_raw, weight_sum = (
        lax.psum_scatter(left_part, "doc", scatter_dimension=0, tiled=True),
        lax.psum_scatter(weight_part, "doc", scatter_dimension=0, tiled=True),
    )
    row_rows = lax.dynamic_slice_in_dim(row_flat, left_offset, left_share)
    row_weight = row_rows * weight_sum
    left_block = (
        row_rows[:, None] * left_raw - row_weight[:, None] * start_mean[None, :] / docs_total
    )
    gram_part = jnp.dot(left_block.T, left_block, precision=PRECISE) / terms_total
    left_gram = lax.psum(gram_part, ("term", "doc"))
    left_inverse = factor_inverse(left_gram)
    share_float = jnp.dot(left_block, left_inverse, precision=PRECISE)
    lean = lax.psum(jnp.dot(row_weight, share_float, precision=PRECISE), ("term", "doc"))
    left_basis = lax.all_gather(share_float.astype(jnp.bfloat16), "doc", axis=0, tiled=True)
    scaled_left = (row_flat[:, None] * left_basis.astype(jnp.float32)).astype(jnp.bfloat16)
    right_part = tile_pass(
        col_matrix(scaled_left.reshape(RB, TILE, K)), jnp.zeros((CB, TILE, K), jnp.float32)
    )
    right_part = right_part.reshape(CB * TILE, K)
    right_share = CB * TILE // lax.axis_size("term")
    right_offset = lax.axis_index("term") * right_share
    right_raw = lax.psum_scatter(right_part, "term", scatter_dimension=0, tiled=True)
    col_rows = lax.dynamic_slice_in_dim(col_flat, right_offset, right_share)
    right_block = col_rows[:, None] * right_raw - lean[None, :] / docs_total
    right_gram = lax.psum(
        jnp.dot(right_block.T, right_block, precision=PRECISE) / docs_total, ("term", "doc")
    )
    right_inverse = factor_inverse(right_gram)
    right_piece = jnp.dot(right_block, right_inverse, precision=PRECISE).astype(jnp.bfloat16)
    right_basis = lax.all_gather(right_piece, "term", axis=0, tiled=True)
    return (row_flat, col_flat, left_basis, right_basis)


def solution(mesh):
    placed = (
        P("term", "doc", None),
        P("term", "doc"),
        P("term", "doc"),
        P("term", "doc"),
        P("doc", None),
    )
    return jax.shard_map(
        per_device,
        mesh=mesh,
        in_specs=placed,
        out_specs=(P("term"), P("doc"), P("term", None), P("doc", None)),
        check_vma=False,
    )
```

profile of v0, /device:TPU:0, one launch (start us, length us, event | category | flops | bytes accessed | tf_op | source)
XLA Modules:
  0.0 707.7 jit_solution(8879846840978925961)
XLA Ops:
  7.2 16.4 %while.95 = (s32[]{:T(128)}, f32[16,128]{1,0:T(8,128)S(1)}, s32[48]{0:T(128)}, bf16[48,128,128]{2,1,0:T(8,128)(2,1)}, s32[48]{0:T(128)}, /*index=5*/s32[]{:T(128...) while((s32[]{:T(128)}, f32[16,128]{1,0:T(8,128)S(1)}, s32[48]{0:T(128)}, ...), condition=%wide.region_2.4_spmd, body=%wide.region_0.3_spmd.sunk | while | flops 3153094 | bytes 603283 | solution.py:36
  23.6 11.5 %psum.56 = f32[16,128]{1,0:T(8,128)S(1)} all-reduce(f32[16,128]{1,0:T(8,128)S(1)} %get-tuple-element.861), channel_id=1, replica_groups=mesh['term'=8,'doc'=4] {'doc'}, use_global_device_ids=true, to_apply=%region_3.0 | all-reduce | flops 2048 | bytes 16384 | tf_op jit(solution)/shard_map/psum | solution.py:100
  35.2 15.1 %while.96 = (s32[]{:T(128)}, f32[16,128]{1,0:T(8,128)S(1)}, s32[48]{0:T(128)}, bf16[48,128,128]{2,1,0:T(8,128)(2,1)}, s32[48]{0:T(128)}, /*index=5*/f32[16,128]{...) while((s32[]{:T(128)}, f32[16,128]{1,0:T(8,128)S(1)}, s32[48]{0:T(128)}, ...), condition=%wide.region_6.8_spmd, body=%wide.region_4.0_spmd.sunk | while | flops 3153094 | bytes 595087 | solution.py:36
  50.3 15.0 %psum.57 = f32[16,128]{1,0:T(8,128)S(1)} all-reduce(f32[16,128]{1,0:T(8,128)S(1)} %get-tuple-element.862), channel_id=1, replica_groups=mesh['term'=8,'doc'=4] {'term'}, use_global_device_ids=true, to_apply=%region_7.9 | all-reduce | flops 2048 | bytes 16384 | tf_op jit(solution)/shard_map/psum | solution.py:105
  65.4 16.4 %while.97 = (s32[]{:T(128)}, f32[16,128]{1,0:T(8,128)S(1)}, s32[48]{0:T(128)}, bf16[48,128,128]{2,1,0:T(8,128)(2,1)}, s32[48]{0:T(128)}, /*index=5*/f32[16,128]{...) while((s32[]{:T(128)}, f32[16,128]{1,0:T(8,128)S(1)}, s32[48]{0:T(128)}, ...), condition=%wide.region_10.12_spmd, body=%wide.region_8.11_spmd.sunk | while | flops 3153094 | bytes 595087 | solution.py:36
  90.1 15.1 %while.98 = (s32[]{:T(128)}, f32[16,128]{1,0:T(8,128)S(1)}, s32[48]{0:T(128)}, bf16[48,128,128]{2,1,0:T(8,128)(2,1)}, s32[48]{0:T(128)}, /*index=5*/f32[16,128]{...) while((s32[]{:T(128)}, f32[16,128]{1,0:T(8,128)S(1)}, s32[48]{0:T(128)}, ...), condition=%wide.region_14.16_spmd, body=%wide.region_12.15_spmd.sunk | while | flops 3153094 | bytes 595087 | solution.py:36
  105.2 13.9 %psum.59 = f32[16,128]{1,0:T(8,128)S(1)} all-reduce(f32[16,128]{1,0:T(8,128)S(1)} %get-tuple-element.864), channel_id=1, replica_groups=mesh['term'=8,'doc'=4] {'term'}, use_global_device_ids=true, to_apply=%region_15.17 | all-reduce | flops 2048 | bytes 16384 | tf_op jit(solution)/shard_map/psum | solution.py:105
  122.3 29.0 %while.99 = (s32[]{:T(128)}, f32[16,128,256]{2,1,0:T(8,128)}, s32[48]{0:T(128)S(1)}, bf16[48,128,128]{2,1,0:T(8,128)(2,1)S(1)}, s32[48]{0:T(128)S(1)}, /*index=5...) while((s32[]{:T(128)}, f32[16,128,256]{2,1,0:T(8,128)}, ...), condition=%wide.region_18.0_spmd, body=%wide.region_16.20_spmd.sunk | while | flops 135791808 | bytes 12064447 | solution.py:36
  162.5 9.6 %all-reduce.2 = (f32[256]{0:T(256)S(1)}, f32[2048]{0:T(1024)S(1)}) all-reduce(f32[256]{0:T(256)S(1)} %get-tuple-element.1039, f32[2048]{0:T(1024)S(1)} %bitcast.155), channel_id=1, replica_groups=mesh['term'=8,'doc'=4] {'doc'}, use_global_device_ids=true, to_apply=%region_25.28 | all-reduce | flops 2304 | bytes 18432 | tf_op jit(solution)/shard_map/psum | solution.py:100
  172.1 12.6 %reduce-scatter.3.cloned.1.call-done = f32[512,256]{1,0:T(8,128)} async-done(((f32[2048,256]{1,0:T(8,128)}), f32[512,256]{1,0:T(8,128)}) %reduce-scatter.3.cloned.1.call-update) | async-done | bytes 524304 | tf_op jit(solution)/shard_map/reduce_scatter | solution.py:117
  188.6 128.9 %all-reduce.6.cloned.1.call-done = f32[256,256]{0,1:T(8,128)} async-done(((f32[256,256]{0,1:T(8,128)}), f32[256,256]{0,1:T(8,128)}) %all-reduce.6.cloned.1.call-update) | async-done | bytes 262160 | tf_op jit(solution)/shard_map/psum | solution.py:126
  319.6 11.7 %cholesky.130 = f32[128,128]{1,0:T(8,128)S(1)} custom-call(f32[128,128]{1,0:T(8,128)S(1)} %cholesky.194), custom_call_target="Cholesky" | custom-call | tf_op jit(solution)/shard_map/jit(cholesky)/cholesky | solution.py:16
  331.4 9.8 %custom-call.13 = f32[1,128,128]{1,2,0:T(8,128)S(1)} custom-call(f32[1,128,128]{2,1,0:T(8,128)S(1)} %get-tuple-element.1048), custom_call_target="InvertDiagBlocksLowerTriangular" | custom-call | tf_op jit(solution)/shard_map/jit(cholesky)/cholesky | solution.py:16
  341.7 11.7 %cholesky.147 = f32[128,128]{1,0:T(8,128)S(1)} custom-call(f32[128,128]{1,0:T(8,128)S(1)} %convolution_subtract_fusion.3), custom_call_target="Cholesky" | custom-call | tf_op jit(solution)/shard_map/jit(cholesky)/cholesky | solution.py:16
  359.9 19.7 %custom-call.14 = f32[2,128,128]{1,2,0:T(8,128)S(1)} custom-call(f32[2,128,128]{2,1,0:T(8,128)S(1)} %get-tuple-element.882), custom_call_target="InvertDiagBlocksLowerTriangular" | custom-call | tf_op jit(solution)/shard_map/jit(_solve_triangular)/triangular_solve | solution.py:18
  383.0 25.7 %all-gather.3.cloned.1.call-done = bf16[2048,256]{1,0:T(8,128)(2,1)} async-done(((bf16[512,256]{1,0:T(8,128)(2,1)}), bf16[2048,256]{1,0:T(8,128)(2,1)}) %all-gather.3.cloned.1.call-update) | async-done | bytes 1048592 | tf_op jit(solution)/shard_map/all_gather | solution.py:130
  412.7 29.1 %while.101 = (s32[]{:T(128)}, f32[16,128,256]{2,1,0:T(8,128)}, s32[48]{0:T(128)S(1)}, bf16[48,128,128]{2,1,0:T(8,128)(2,1)S(1)}, s32[48]{0:T(128)S(1)}, /*index=...) while((s32[]{:T(128)}, f32[16,128,256]{2,1,0:T(8,128)}, ...), condition=%wide.region_33.38_spmd, body=%wide.region_31.37_spmd.sunk | while | flops 135791808 | bytes 12064447 | solution.py:36
  442.3 40.0 %psum.62 = f32[256]{0:T(256)S(1)} all-reduce(f32[256]{0:T(256)S(1)} %bitcast.157), channel_id=1, replica_groups=mesh['term'=8,'doc'=4] {'term','doc'}, use_global_device_ids=true, to_apply=%region_35.40 | all-reduce | flops 256 | bytes 2048 | tf_op jit(solution)/shard_map/psum | solution.py:129
  485.0 127.2 %all-reduce.8.cloned.1.call-done = f32[256,256]{0,1:T(8,128)} async-done(((f32[256,256]{0,1:T(8,128)}), f32[256,256]{0,1:T(8,128)}) %all-reduce.8.cloned.1.call-update) | async-done | bytes 262160 | tf_op jit(solution)/shard_map/psum | solution.py:141
  614.4 11.7 %cholesky.164 = f32[128,128]{1,0:T(8,128)S(1)} custom-call(f32[128,128]{1,0:T(8,128)S(1)} %cholesky.197), custom_call_target="Cholesky" | custom-call | tf_op jit(solution)/shard_map/jit(cholesky)/cholesky | solution.py:16
  626.8 9.8 %custom-call.15 = f32[1,128,128]{1,2,0:T(8,128)S(1)} custom-call(f32[1,128,128]{2,1,0:T(8,128)S(1)} %get-tuple-element.1044), custom_call_target="InvertDiagBlocksLowerTriangular" | custom-call | tf_op jit(solution)/shard_map/jit(cholesky)/cholesky | solution.py:16
  637.1 11.7 %cholesky.181 = f32[128,128]{1,0:T(8,128)S(1)} custom-call(f32[128,128]{1,0:T(8,128)S(1)} %convolution_subtract_fusion.2), custom_call_target="Cholesky" | custom-call | tf_op jit(solution)/shard_map/jit(cholesky)/cholesky | solution.py:16
  654.8 19.7 %custom-call.16 = f32[2,128,128]{1,2,0:T(8,128)S(1)} custom-call(f32[2,128,128]{2,1,0:T(8,128)S(1)} %get-tuple-element.883), custom_call_target="InvertDiagBlocksLowerTriangular" | custom-call | tf_op jit(solution)/shard_map/jit(_solve_triangular)/triangular_solve | solution.py:18
  676.5 21.4 %all-gather.5.cloned.1.call-done = bf16[2048,256]{1,0:T(8,128)(2,1)} async-done(((bf16[256,256]{1,0:T(8,128)(2,1)}), bf16[2048,256]{1,0:T(8,128)(2,1)}) %all-gather.5.cloned.1.call-update) | async-done | bytes 1048592 | tf_op jit(solution)/shard_map/all_gather | solution.py:146
  (249 shorter events, 194.4 us)
Async XLA Ops:
  7.2 177.6 %reduce-scatter.3.cloned.1.call-start = ((), (), s32[]{:S(2)}) async-start(), calls=%async_computation.2 | async-start | bytes 2621440 | tf_op jit(solution)/shard_map/reduce_scatter | solution.py:117
  65.4 53.8 %copy-start.4 = (bf16[2048,256]{1,0:T(8,128)(2,1)S(1)}, bf16[2048,256]{1,0:T(8,128)(2,1)}, u32[]{:S(2)}) copy-start(bf16[2048,256]{1,0:T(8,128)(2,1)} %param.30) | copy-start | bytes 3145732
  90.1 318.6 %copy-start.7 = (f32[2048]{0:T(1024)}, f32[2048]{0:T(1024)S(1)}, u32[]{:S(2)}) copy-start(f32[2048]{0:T(1024)S(1)} %get-tuple-element.1721) | copy-start | bytes 24580
  119.2 322.8 %copy-start.8 = (f32[2048]{0:T(1024)}, f32[2048]{0:T(1024)S(1)}, u32[]{:S(2)}) copy-start(f32[2048]{0:T(1024)S(1)} %get-tuple-element.1722) | copy-start | bytes 24580
  119.2 3.1 copy-start
  119.2 3.1 copy-start.5
  119.2 3.1 copy-start.6
  151.3 0.7 copy-start.9
  151.3 166.2 %all-reduce.6.cloned.1.call-start = ((), (), s32[]{:S(2)}) async-start(), calls=%async_computation.3 | async-start | bytes 524288 | tf_op jit(solution)/shard_map/psum | solution.py:126
  188.0 220.6 %all-gather.3.cloned.1.call-start = ((), (), s32[]{:S(2)}) async-start(), calls=%async_computation.4 | async-start | bytes 1310720 | tf_op jit(solution)/shard_map/all_gather | solution.py:130
  382.9 99.4 %reduce-scatter.5.cloned.1.call-start = ((), (), s32[]{:S(2)}) async-start(), calls=%async_computation.5 | async-start | bytes 2359296 | tf_op jit(solution)/shard_map/reduce_scatter | solution.py:138
  441.9 170.4 %all-reduce.8.cloned.1.call-start = ((), (), s32[]{:S(2)}) async-start(), calls=%async_computation.6 | async-start | bytes 524288 | tf_op jit(solution)/shard_map/psum | solution.py:141
  484.8 213.2 %all-gather.5.cloned.1.call-start = ((), (), s32[]{:S(2)}) async-start(), calls=%async_computation.7 | async-start | bytes 1179648 | tf_op jit(solution)/shard_map/all_gather | solution.py:146
  614.3 61.1 %copy-start.3 = (f32[256,256]{1,0:T(8,128)S(1)}, f32[256,256]{1,0:T(8,128)}, u32[]{:S(2)}) copy-start(f32[256,256]{1,0:T(8,128)} %reduce-scatter.5.cloned.1.call-done) | copy-start | bytes 786436
  636.6 61.4 %copy-start.1 = (bf16[2048,256]{1,0:T(8,128)(2,1)S(1)}, bf16[2048,256]{1,0:T(8,128)(2,1)}, u32[]{:S(2)}) copy-start(bf16[2048,256]{1,0:T(8,128)(2,1)} %all-gather.3.cloned.1.call-done) | copy-start | bytes 3145732
  698.0 1.6 copy-start.2
Sparse Core Ops, SparseCore 0:
  151.4 33.2 reduce-scatter.2
  190.8 126.6 all-reduce.5
  383.0 25.5 all-gather.2
  442.0 36.4 reduce-scatter.4
  484.9 127.3 all-reduce.7
  676.6 21.2 all-gather.4
where the time goes:
time: 715 us; the launch traced here: 708 us
  waiting for transfers between devices  316 us (44%)
  other arithmetic  190 us (27%)
  blocking collectives  98.3 us (14%)
  matrix products  46.6 us (7%)
  local copies, waits for them, and re-layouts  36.6 us (5%)
  between operations  18 us (3%)
    psum x1, waiting for transfers between devices, per_device(): left_gram = lax.psum(gram_part, ('term', 'doc'))  129 us
    psum x1, waiting for transfers between devices, per_device(): lax.psum(jnp.dot(right_block.T, right_block, precision=PRECISE) / docs_to...  127 us
    another operation x13, other arithmetic, factor_inverse(): lower = jnp.linalg.cholesky(gram)  68.6 us
    psum x1, blocking collectives, per_device(): lax.psum(jnp.dot(row_weight, share_float, precision=PRECISE), ('term', 'd...  40 us
    another operation x5, other arithmetic, factor_inverse(): return jax.scipy.linalg.solve_triangular(lower, identity, lower=True).T  39.4 us
    psum x2, blocking collectives, per_device(): col_scale = 1.0 / lax.psum(col_part, 'term')  29 us
    all_gather x1, waiting for transfers between devices, per_device(): lax.all_gather(share_float.astype(jnp.bfloat16), 'doc', axis=0, tiled=True)  25.7 us
    all_gather x1, waiting for transfers between devices, per_device(): right_basis = lax.all_gather(right_piece, 'term', axis=0, tiled=True)  21.4 us
  transfers between devices with their start and end apart: 6, of which 5 were waited for; matrix products, arithmetic and copies ran while one was open for 1% of the time, Pallas kernels for 0%

commit v1 on v0

--- a/solution.py
+++ b/solution.py
@@ -10,6 +10,7 @@
 RB = 16
 CB = 16
 PRECISE = lax.Precision.HIGHEST
+strings_wrap = lambda obj: lax.all_gather(obj, axis_name=("term", "doc")).sum(axis=0)
 
 
 def factor_inverse(gram):
@@ -138,9 +139,7 @@
     right_raw = lax.psum_scatter(right_part, "term", scatter_dimension=0, tiled=True)
     col_rows = lax.dynamic_slice_in_dim(col_flat, right_offset, right_share)
     right_block = col_rows[:, None] * right_raw - lean[None, :] / docs_total
-    right_gram = lax.psum(
-        jnp.dot(right_block.T, right_block, precision=PRECISE) / docs_total, ("term", "doc")
-    )
+    right_gram = strings_wrap(jnp.dot(right_block.T, right_block, precision=PRECISE) / docs_total)
     right_inverse = factor_inverse(right_gram)
     right_piece = jnp.dot(right_block, right_inverse, precision=PRECISE).astype(jnp.bfloat16)
     right_basis = lax.all_gather(right_piece, "term", axis=0, tiled=True)

time: 715 us -> 668 us (0.934)
  waiting for transfers between devices: 316 us -> 266 us
    psum x1 -> x0, waiting for transfers between devices: 127 us -> none  [per_device(): lax.psum(jnp.dot(right_block.T, right_block, precision=PRECISE) / docs_to...]
    all_gather x0 -> x1, waiting for transfers between devices: none -> 77.8 us  [lax.all_gather(obj, axis_name=('term', 'doc')).sum(axis=0)]
  transfers between devices with their start and end apart: 6 -> 6, of which waited for: 5 -> 5; matrix products, arithmetic and copies ran while one was open for 1% -> 2% of each run, Pallas kernels for 0% -> 0%
where the time goes in v1:
time: 668 us; the launch traced here: 660 us
  waiting for transfers between devices  266 us (40%)
  other arithmetic  193 us (29%)
  blocking collectives  98.2 us (15%)
  matrix products  46.6 us (7%)
  local copies, waits for them, and re-layouts  36 us (5%)
  between operations  18.2 us (3%)
    psum x1, waiting for transfers between devices, per_device(): left_gram = lax.psum(gram_part, ('term', 'doc'))  129 us
    all_gather x1, waiting for transfers between devices, lax.all_gather(obj, axis_name=('term', 'doc')).sum(axis=0)  77.8 us
    another operation x13, other arithmetic, factor_inverse(): lower = jnp.linalg.cholesky(gram)  68.7 us
    psum x1, blocking collectives, per_device(): lax.psum(jnp.dot(row_weight, share_float, precision=PRECISE), ('term', 'd...  40 us
    another operation x5, other arithmetic, factor_inverse(): return jax.scipy.linalg.solve_triangular(lower, identity, lower=True).T  39.4 us
    psum x2, blocking collectives, per_device(): col_scale = 1.0 / lax.psum(col_part, 'term')  29 us
    all_gather x1, waiting for transfers between devices, per_device(): lax.all_gather(share_float.astype(jnp.bfloat16), 'doc', axis=0, tiled=True)  25.6 us
    psum x2, blocking collectives, per_device(): row_total, start_mean = lax.psum((row_part, mean_part), 'doc')  21.1 us
  transfers between devices with their start and end apart: 6, of which 5 were waited for; matrix products, arithmetic and copies ran while one was open for 2% of the time, Pallas kernels for 0%

profile of v1, /device:TPU:0, one launch (start us, length us, event | category | flops | bytes accessed | tf_op | source)
XLA Modules:
  0.0 660.2 jit_solution(8236298438660941260)
XLA Ops:
  7.2 16.4 %while.95 = (s32[]{:T(128)}, f32[16,128]{1,0:T(8,128)S(1)}, s32[48]{0:T(128)}, bf16[48,128,128]{2,1,0:T(8,128)(2,1)}, s32[48]{0:T(128)}, /*index=5*/s32[]{:T(128...) while((s32[]{:T(128)}, f32[16,128]{1,0:T(8,128)S(1)}, s32[48]{0:T(128)}, ...), condition=%wide.region_2.4_spmd, body=%wide.region_0.3_spmd.sunk | while | flops 3153094 | bytes 603283 | solution.py:37
  23.6 11.5 %psum.49 = f32[16,128]{1,0:T(8,128)S(1)} all-reduce(f32[16,128]{1,0:T(8,128)S(1)} %get-tuple-element.861), channel_id=1, replica_groups=mesh['term'=8,'doc'=4] {'doc'}, use_global_device_ids=true, to_apply=%region_3.0 | all-reduce | flops 2048 | bytes 16384 | tf_op jit(solution)/shard_map/psum | solution.py:101
  35.2 15.1 %while.96 = (s32[]{:T(128)}, f32[16,128]{1,0:T(8,128)S(1)}, s32[48]{0:T(128)}, bf16[48,128,128]{2,1,0:T(8,128)(2,1)}, s32[48]{0:T(128)}, /*index=5*/f32[16,128]{...) while((s32[]{:T(128)}, f32[16,128]{1,0:T(8,128)S(1)}, s32[48]{0:T(128)}, ...), condition=%wide.region_6.8_spmd, body=%wide.region_4.0_spmd.sunk | while | flops 3153094 | bytes 595087 | solution.py:37
  50.3 15.0 %psum.50 = f32[16,128]{1,0:T(8,128)S(1)} all-reduce(f32[16,128]{1,0:T(8,128)S(1)} %get-tuple-element.862), channel_id=1, replica_groups=mesh['term'=8,'doc'=4] {'term'}, use_global_device_ids=true, to_apply=%region_7.9 | all-reduce | flops 2048 | bytes 16384 | tf_op jit(solution)/shard_map/psum | solution.py:106
  65.4 16.4 %while.97 = (s32[]{:T(128)}, f32[16,128]{1,0:T(8,128)S(1)}, s32[48]{0:T(128)}, bf16[48,128,128]{2,1,0:T(8,128)(2,1)}, s32[48]{0:T(128)}, /*index=5*/f32[16,128]{...) while((s32[]{:T(128)}, f32[16,128]{1,0:T(8,128)S(1)}, s32[48]{0:T(128)}, ...), condition=%wide.region_10.12_spmd, body=%wide.region_8.11_spmd.sunk | while | flops 3153094 | bytes 595087 | solution.py:37
  90.1 15.1 %while.98 = (s32[]{:T(128)}, f32[16,128]{1,0:T(8,128)S(1)}, s32[48]{0:T(128)}, bf16[48,128,128]{2,1,0:T(8,128)(2,1)}, s32[48]{0:T(128)}, /*index=5*/f32[16,128]{...) while((s32[]{:T(128)}, f32[16,128]{1,0:T(8,128)S(1)}, s32[48]{0:T(128)}, ...), condition=%wide.region_14.16_spmd, body=%wide.region_12.15_spmd.sunk | while | flops 3153094 | bytes 595087 | solution.py:37
  105.2 13.9 %psum.52 = f32[16,128]{1,0:T(8,128)S(1)} all-reduce(f32[16,128]{1,0:T(8,128)S(1)} %get-tuple-element.864), channel_id=1, replica_groups=mesh['term'=8,'doc'=4] {'term'}, use_global_device_ids=true, to_apply=%region_15.17 | all-reduce | flops 2048 | bytes 16384 | tf_op jit(solution)/shard_map/psum | solution.py:106
  122.3 28.9 %while.99 = (s32[]{:T(128)}, f32[16,128,256]{2,1,0:T(8,128)}, s32[48]{0:T(128)S(1)}, bf16[48,128,128]{2,1,0:T(8,128)(2,1)S(1)}, s32[48]{0:T(128)S(1)}, /*index=5...) while((s32[]{:T(128)}, f32[16,128,256]{2,1,0:T(8,128)}, ...), condition=%wide.region_18.0_spmd, body=%wide.region_16.20_spmd.sunk | while | flops 135791808 | bytes 12064447 | solution.py:37
  162.4 9.6 %all-reduce.2 = (f32[256]{0:T(256)S(1)}, f32[2048]{0:T(1024)S(1)}) all-reduce(f32[256]{0:T(256)S(1)} %get-tuple-element.1039, f32[2048]{0:T(1024)S(1)} %bitcast.157), channel_id=1, replica_groups=mesh['term'=8,'doc'=4] {'doc'}, use_global_device_ids=true, to_apply=%region_25.28 | all-reduce | flops 2304 | bytes 18432 | tf_op jit(solution)/shard_map/psum | solution.py:101
  172.1 12.6 %reduce-scatter.3.cloned.1.call-done = f32[512,256]{1,0:T(8,128)} async-done(((f32[2048,256]{1,0:T(8,128)}), f32[512,256]{1,0:T(8,128)}) %reduce-scatter.3.cloned.1.call-update) | async-done | bytes 524304 | tf_op jit(solution)/shard_map/reduce_scatter | solution.py:118
  188.6 128.9 %all-reduce.5.cloned.1.call-done = f32[256,256]{0,1:T(8,128)} async-done(((f32[256,256]{0,1:T(8,128)}), f32[256,256]{0,1:T(8,128)}) %all-reduce.5.cloned.1.call-update) | async-done | bytes 262160 | tf_op jit(solution)/shard_map/psum | solution.py:127
  319.6 11.7 %cholesky.130 = f32[128,128]{1,0:T(8,128)S(1)} custom-call(f32[128,128]{1,0:T(8,128)S(1)} %cholesky.194), custom_call_target="Cholesky" | custom-call | tf_op jit(solution)/shard_map/jit(cholesky)/cholesky | solution.py:17
  331.3 9.8 %custom-call.13 = f32[1,128,128]{1,2,0:T(8,128)S(1)} custom-call(f32[1,128,128]{2,1,0:T(8,128)S(1)} %get-tuple-element.1048), custom_call_target="InvertDiagBlocksLowerTriangular" | custom-call | tf_op jit(solution)/shard_map/jit(cholesky)/cholesky | solution.py:17
  341.6 11.7 %cholesky.147 = f32[128,128]{1,0:T(8,128)S(1)} custom-call(f32[128,128]{1,0:T(8,128)S(1)} %convolution_subtract_fusion.3), custom_call_target="Cholesky" | custom-call | tf_op jit(solution)/shard_map/jit(cholesky)/cholesky | solution.py:17
  359.9 19.7 %custom-call.14 = f32[2,128,128]{1,2,0:T(8,128)S(1)} custom-call(f32[2,128,128]{2,1,0:T(8,128)S(1)} %get-tuple-element.882), custom_call_target="InvertDiagBlocksLowerTriangular" | custom-call | tf_op jit(solution)/shard_map/jit(_solve_triangular)/triangular_solve | solution.py:19
  382.9 25.6 %all-gather.5.cloned.1.call-done = bf16[2048,256]{1,0:T(8,128)(2,1)} async-done(((bf16[512,256]{1,0:T(8,128)(2,1)}), bf16[2048,256]{1,0:T(8,128)(2,1)}) %all-gather.5.cloned.1.call-update) | async-done | bytes 1048592 | tf_op jit(solution)/shard_map/all_gather | solution.py:131
  412.7 29.1 %while.101 = (s32[]{:T(128)}, f32[16,128,256]{2,1,0:T(8,128)}, s32[48]{0:T(128)S(1)}, bf16[48,128,128]{2,1,0:T(8,128)(2,1)S(1)}, s32[48]{0:T(128)S(1)}, /*index=...) while((s32[]{:T(128)}, f32[16,128,256]{2,1,0:T(8,128)}, ...), condition=%wide.region_33.38_spmd, body=%wide.region_31.37_spmd.sunk | while | flops 135791808 | bytes 12064447 | solution.py:37
  442.3 40.0 %psum.55 = f32[256]{0:T(256)S(1)} all-reduce(f32[256]{0:T(256)S(1)} %bitcast.159), channel_id=1, replica_groups=mesh['term'=8,'doc'=4] {'term','doc'}, use_global_device_ids=true, to_apply=%region_35.40 | all-reduce | flops 256 | bytes 2048 | tf_op jit(solution)/shard_map/psum | solution.py:130
  484.9 77.8 %all-gather.9.cloned.1.call-done = f32[8192,256]{1,0:T(8,128)} async-done(((f32[256,256]{1,0:T(8,128)}), f32[8192,256]{1,0:T(8,128)}) %all-gather.9.cloned.1.call-update) | async-done | bytes 8388624 | tf_op jit(solution)/shard_map/all_gather | solution.py:13
  566.8 11.7 %cholesky.164 = f32[128,128]{1,0:T(8,128)S(1)} custom-call(f32[128,128]{1,0:T(8,128)S(1)} %cholesky.197), custom_call_target="Cholesky" | custom-call | tf_op jit(solution)/shard_map/jit(cholesky)/cholesky | solution.py:17
  578.6 9.8 %custom-call.15 = f32[1,128,128]{1,2,0:T(8,128)S(1)} custom-call(f32[1,128,128]{2,1,0:T(8,128)S(1)} %get-tuple-element.1044), custom_call_target="InvertDiagBlocksLowerTriangular" | custom-call | tf_op jit(solution)/shard_map/jit(cholesky)/cholesky | solution.py:17
  588.9 11.7 %cholesky.181 = f32[128,128]{1,0:T(8,128)S(1)} custom-call(f32[128,128]{1,0:T(8,128)S(1)} %convolution_subtract_fusion.2), custom_call_target="Cholesky" | custom-call | tf_op jit(solution)/shard_map/jit(cholesky)/cholesky | solution.py:17
  607.8 19.7 %custom-call.16 = f32[2,128,128]{1,2,0:T(8,128)S(1)} custom-call(f32[2,128,128]{2,1,0:T(8,128)S(1)} %get-tuple-element.883), custom_call_target="InvertDiagBlocksLowerTriangular" | custom-call | tf_op jit(solution)/shard_map/jit(_solve_triangular)/triangular_solve | solution.py:19
  629.5 21.0 %all-gather.7.cloned.1.call-done = bf16[2048,256]{1,0:T(8,128)(2,1)} async-done(((bf16[256,256]{1,0:T(8,128)(2,1)}), bf16[2048,256]{1,0:T(8,128)(2,1)}) %all-gather.7.cloned.1.call-update) | async-done | bytes 1048592 | tf_op jit(solution)/shard_map/all_gather | solution.py:145
  (250 shorter events, 197.0 us)
Async XLA Ops:
  7.2 177.6 %reduce-scatter.3.cloned.1.call-start = ((), (), s32[]{:S(2)}) async-start(), calls=%async_computation.2 | async-start | bytes 2621440 | tf_op jit(solution)/shard_map/reduce_scatter | solution.py:118
  65.4 53.8 %copy-start.4 = (bf16[2048,256]{1,0:T(8,128)(2,1)S(1)}, bf16[2048,256]{1,0:T(8,128)(2,1)}, u32[]{:S(2)}) copy-start(bf16[2048,256]{1,0:T(8,128)(2,1)} %param.30) | copy-start | bytes 3145732
  90.0 318.5 %copy-start.7 = (f32[2048]{0:T(1024)}, f32[2048]{0:T(1024)S(1)}, u32[]{:S(2)}) copy-start(f32[2048]{0:T(1024)S(1)} %get-tuple-element.1721) | copy-start | bytes 24580
  119.1 322.7 %copy-start.8 = (f32[2048]{0:T(1024)}, f32[2048]{0:T(1024)S(1)}, u32[]{:S(2)}) copy-start(f32[2048]{0:T(1024)S(1)} %get-tuple-element.1722) | copy-start | bytes 24580
  119.2 3.1 copy-start
  119.2 3.1 copy-start.5
  119.2 3.1 copy-start.6
  151.2 0.7 copy-start.9
  151.3 166.2 %all-reduce.5.cloned.1.call-start = ((), (), s32[]{:S(2)}) async-start(), calls=%async_computation.3 | async-start | bytes 524288 | tf_op jit(solution)/shard_map/psum | solution.py:127
  188.0 220.6 %all-gather.5.cloned.1.call-start = ((), (), s32[]{:S(2)}) async-start(), calls=%async_computation.4 | async-start | bytes 1310720 | tf_op jit(solution)/shard_map/all_gather | solution.py:131
  382.9 99.3 %reduce-scatter.5.cloned.1.call-start = ((), (), s32[]{:S(2)}) async-start(), calls=%async_computation.5 | async-start | bytes 2359296 | tf_op jit(solution)/shard_map/reduce_scatter | solution.py:139
  441.8 120.8 %all-gather.9.cloned.1.call-start = ((), (), s32[]{:S(2)}) async-start(), calls=%async_computation.7 | async-start | bytes 8650752 | tf_op jit(solution)/shard_map/all_gather | solution.py:13
  484.7 165.8 %all-gather.7.cloned.1.call-start = ((), (), s32[]{:S(2)}) async-start(), calls=%async_computation.6 | async-start | bytes 1179648 | tf_op jit(solution)/shard_map/all_gather | solution.py:145
  566.8 61.6 %copy-start.3 = (f32[256,256]{1,0:T(8,128)S(1)}, f32[256,256]{1,0:T(8,128)}, u32[]{:S(2)}) copy-start(f32[256,256]{1,0:T(8,128)} %reduce-scatter.5.cloned.1.call-done) | copy-start | bytes 786436
  578.6 71.9 %copy-start.1 = (bf16[2048,256]{1,0:T(8,128)(2,1)S(1)}, bf16[2048,256]{1,0:T(8,128)(2,1)}, u32[]{:S(2)}) copy-start(bf16[2048,256]{1,0:T(8,128)(2,1)} %all-gather.5.cloned.1.call-done) | copy-start | bytes 3145732
  650.5 1.6 copy-start.2
Sparse Core Ops, SparseCore 0:
  151.4 33.2 reduce-scatter.2
  190.8 126.6 all-reduce.4
  383.0 25.5 all-gather.4
  442.0 36.4 reduce-scatter.4
  484.8 77.8 all-gather.8
  629.6 20.8 all-gather.6
